TPU v7x, 32 devices: a whole 2x2x4 slice. The times are simulated.
32 devices in a mesh: section: 4 (over y, core), chan: 8 (over z, x).
Axes of the slice: x: 2, y: 2, z: 4, core: 2. Of those that a mesh axis runs over, the one named last changes fastest.
Arguments:
- raw_traces: bfloat16 [2048, 1024], P(('section', 'chan')), may hold values from -6 to 6
- fir_taps: bfloat16 [64], replicated, may hold values from -0.75 to 0.75
- space_taps: float32 [33], replicated, may hold values from -1 to 1
- source_index: int32 [4, 96], P('section', 'chan'), may hold values from 0 to 511, as said below
Outputs:
- gathers: bfloat16 [2048, 64, 96], P(('section', 'chan'))
Inputs may be any that keep to these rules, and one draw needn't show every extreme that they name: `source_index`: entries j * 12 to (j + 1) * 12 - 1 of a section's row are distinct and lie in channels j * 64 to (j + 1) * 64 - 1; the first such block of every section names channel 0 and the last names channel 512 - 1.
All inputs are finite; a program needn't handle non-finite values.
Results may differ from a plain program's by a relative error of at most 0.0058.
Values may be sent and summed in bfloat16 or wider, within the bound.
A program may use at most 64 MiB of HBM per device.

v0:
```python
import jax
import jax.numpy as jnp
from jax import lax
from jax.sharding import PartitionSpec as P

LAGS = 64


def extended(x, sides, width):
    for axis, dim in sides:
        size, length = (lax.axis_size(axis), x.shape[dim])
        up = [(i, (i + 1) % size) for i in range(size - 1)]
        down = [(j, i) for i, j in up]
        last = lax.slice_in_dim(x, length - width, length, axis=dim)
        leading = lax.slice_in_dim(x, 0, width, axis=dim)
        before = lax.ppermute(last, axis, up)
        after = lax.ppermute(leading, axis, down)
        x = jnp.concatenate([before, x, after], axis=dim)
    return x


def fir_matrix(taps, length):
    count = taps.shape[0]
    lead = jnp.zeros((length - 1,), taps.dtype)
    tail = jnp.zeros((length + 1 - count,), taps.dtype)
    period = jnp.concatenate([lead, taps, tail])
    flat = jnp.tile(period, length)[: length * (2 * length - 1)]
    return flat.reshape(length, 2 * length - 1)[:, length - 1 :]


def space_filter(padded, space_taps, rows):
    total = jnp.zeros((rows, padded.shape[1]), jnp.float32)
    for offset in range(space_taps.shape[0]):
        total = total + space_taps[offset] * padded[offset : offset + rows].astype(jnp.float32)
    return total.astype(jnp.bfloat16)


def correlate(receivers, sources):
    rows, length = receivers.shape
    blocks = []
    for first in range(0, LAGS, 8):
        shifted = []
        for lag in range(first, first + 8):
            shifted.append(jnp.pad(receivers[:, lag:], ((0, 0), (0, lag))))
        stacked = jnp.stack(shifted, axis=1).reshape(rows * 8, length)
        block = lax.dot_general(
            stacked, sources, (((1,), (1,)), ((), ())), preferred_element_type=jnp.float32
        )
        blocks.append(block.reshape(rows, 8, sources.shape[0]))
    joined = jnp.concatenate(blocks, axis=1)
    return (joined * (1.0 / length**0.5)).astype(jnp.bfloat16)


def shards(raw_traces, fir_taps, space_taps, source_index):
    rows, length = raw_traces.shape
    banded = jnp.dot(
        raw_traces, fir_matrix(fir_taps, length), preferred_element_type=jnp.float32
    ).astype(jnp.bfloat16)
    half = (space_taps.shape[0] - 1) // 2
    padded = extended(banded, ((("section", "chan"), 0),), half)
    filtered = space_filter(padded, space_taps, rows)
    whole_traces, whole_index = (
        lax.all_gather(filtered, "chan", axis=0, tiled=True),
        lax.all_gather(source_index, "chan", axis=1, tiled=True),
    )
    sources = jnp.take(whole_traces, whole_index[0], axis=0)
    return correlate(filtered, sources)


def solution(mesh):
    return jax.shard_map(
        shards,
        mesh=mesh,
        in_specs=(P(("section", "chan"), None), P(), P(), P("section", "chan")),
        out_specs=P(("section", "chan"), None, None),
        check_vma=False,
    )
```

profile of v0, /device:TPU:1, one launch (start us, length us, event | category | flops | bytes accessed | tf_op | source)
XLA Modules:
  0.0 130.7 jit_solution(16714103273075158136)
XLA Ops:
  6.5 0.8 concatenate.43
  7.3 1.0 broadcast_bitcast_fusion
  8.4 1.4 %copy.29 = bf16[128,16,8,128]{3,1,2,0:T(8,128)(2,1)S(1)} copy(bf16[128,16,8,128]{3,2,1,0:T(8,128)(2,1)S(1)} %broadcast_bitcast_fusion) | data formatting | bytes 8388608
  9.8 2.2 %slice.562 = bf16[2096128]{0:T(1024)(128)(2,1)} slice(bf16[2097152]{0:T(1024)(128)(2,1)S(1)} %bitcast.199), slice={[0:2096128]} | slice | bytes 8384512 | tf_op jit(solution)/shard_map/slice | solution.py:27
  12.0 10.7 %reshape.70 = bf16[1024,2047]{1,0:T(8,128)(2,1)} reshape(bf16[2096128]{0:T(1024)(128)(2,1)} %slice.562) | data formatting | bytes 8384512 | tf_op jit(solution)/shard_map/reshape | solution.py:28
  22.7 2.5 %fusion.5 = bf16[64,1024]{1,0:T(8,128)(2,1)S(1)} fusion(bf16[64,1024]{1,0:T(8,128)(2,1)S(1)} %copy-done, bf16[1024,2047]{1,0:T(8,128)(2,1)} %reshape.70), kind=kOutput, calls=%fused_computation.6 | convolution fusion | flops 134283264 | bytes 2359296 | tf_op jit(solution)/shard_map/dot_general | solution.py:56
  25.2 7.5 %collective-permute-start.1 = (bf16[16,1024]{1,0:T(8,128)(2,1)S(1)}, bf16[16,1024]{1,0:T(8,128)(2,1)S(1)}, u32[]{:S(2)}, u32[]{:S(2)}) collective-permute-start(bf16[16,1024]{1,0:T(8,128)(2,1)S(1)} %get-tuple-element.8), channel_id=1, source_target_pairs={{1,0},{2,1},{3,2},{4,3},{5,4},{6,5},{7,6},{8,7},{9,8},{10,9},{11,1... | collective-permute-start | bytes 98312 | tf_op jit(solution)/shard_map/ppermute | solution.py:17
  32.8 1.9 %collective-permute-start = (bf16[16,1024]{1,0:T(8,128)(2,1)S(1)}, bf16[16,1024]{1,0:T(8,128)(2,1)S(1)}, u32[]{:S(2)}, u32[]{:S(2)}) collective-permute-start(bf16[16,1024]{1,0:T(8,128)(2,1)S(1)} %get-tuple-element.7), channel_id=1, source_target_pairs={{0,1},{1,2},{2,3},{3,4},{4,5},{5,6},{6,7},{7,8},{8,9},{9,10},{10,1... | collective-permute-start | bytes 98312 | tf_op jit(solution)/shard_map/ppermute | solution.py:16
  34.7 0.7 fusion.57
  35.4 0.7 fusion.56
  37.4 9.3 %all-reduce.63 = s32[96]{0:T(128)S(1)} all-reduce(s32[96]{0:T(128)S(1)} %bitcast_dynamic-update-slice_fusion), channel_id=1, replica_groups=mesh['section'=4,'chan'=8] {'chan'}, use_global_device_ids=true, to_apply=%add.63 | all-reduce | flops 96 | bytes 768 | tf_op jit(solution)/shard_map/squeeze | solution.py:66
  46.7 21.9 %constant_dynamic-update-slice_fusion.7 = (bf16[64,8,1024]{2,0,1:T(8,128)(2,1)S(1)}, bf16[64,1024]{1,0:T(8,128)(2,1)S(1)}) fusion(bf16[16,1024]{1,0:T(8,128)(2,1)S(1)} %collective-permute-done.1, bf16[64,1024]{1,0:T(8,128)(2,1)S(1)} %fusion.5, f32[]{:T(128)} %bitcast.33, f32[]{:T(128)} %bitcast.32, f32[]{:T(128)} %bitcast.31, f32[]{:T(128)} %bitcast.30, ...), kind=kLoop, calls=%fused_computation.70 | loop fusion | flops 12779519 | bytes 458884
  68.6 0.8 slice.626
  69.4 0.8 slice.627
  70.1 0.8 slice.628
  70.9 0.8 slice.629
  71.7 0.8 slice.630
  72.4 0.8 slice.631
  73.2 0.8 slice.632
  74.0 1.1 slice.633
  75.1 1.0 slice.634
  76.1 1.0 slice.635
  77.1 1.0 slice.636
  78.1 1.0 slice.637
  79.1 1.0 slice.638
  80.1 1.0 slice.639
  81.1 1.0 slice.640
  88.7 0.6 copy-done.11
  90.8 22.7 %all-gather.2.cloned.1.call-done = bf16[512,1024]{1,0:T(8,128)(2,1)} async-done(((bf16[64,1024]{1,0:T(8,128)(2,1)}), bf16[512,1024]{1,0:T(8,128)(2,1)}) %all-gather.2.cloned.1.call-update) | async-done | bytes 1048592 | tf_op jit(solution)/shard_map/all_gather | solution.py:63
  113.5 2.3 %gather_fusion = bf16[96,1024]{1,0:T(8,128)(2,1)S(1)} fusion(bf16[512,1024]{1,0:T(8,128)(2,1)} %all-gather.2.cloned.1.call-done, s32[1024]{0:T(1024)S(1)} %pad_clamp_fusion), kind=kCustom, calls=%fused_computation | custom fusion | bytes 393600 | tf_op jit(solution)/shard_map/jit(_take)/gather | solution.py:66
  116.5 1.8 %fusion.20 = f32[64,8,96]{2,0,1:T(8,128)S(1)} fusion(bf16[64,8,1024]{2,0,1:T(8,128)(2,1)} %copy-done.11, bf16[96,1024]{1,0:T(8,128)(2,1)S(1)} %gather_fusion, pred[96]{0:T(512)(128)(4,1)S(1)} %compare_and_fusion), kind=kOutput, calls=%fused_computation.58 | convolution fusion | flops 100761600 | bytes 1441888 | tf_op jit(solution)/shard_map/dot_general | solution.py:46
  122.6 1.2 multiply_convert_fusion
  (182 shorter events, 12.7 us)
Async XLA Ops:
  6.5 16.1 %copy-start = (bf16[64,1024]{1,0:T(8,128)(2,1)S(1)}, bf16[64,1024]{1,0:T(8,128)(2,1)}, u32[]{:S(2)}) copy-start(bf16[64,1024]{1,0:T(8,128)(2,1)} %param.4) | copy-start | bytes 393220
  6.5 107.0 %all-gather.2.cloned.1.call-start = ((), (), s32[]{:S(2)}) async-start(), calls=%async_computation | async-start | bytes 1179648 | tf_op jit(solution)/shard_map/all_gather | solution.py:63
  22.7 12.0 %copy-start.12 = (f32[33]{0:T(128)S(1)}, f32[33]{0:T(128)}, u32[]{:S(2)}) copy-start(f32[33]{0:T(128)} %param.6) | copy-start | bytes 400
  22.7 13.5 %copy-start.21 = (u32[32]{0:T(128)S(1)}, u32[32]{0:T(128)}, u32[]{:S(2)}) copy-start(u32[32]{0:T(128)} %constant.152) | copy-start | bytes 388
  22.7 14.6 %copy-start.20 = (s32[1,12]{1,0:T(1,128)S(1)}, s32[1,12]{1,0:T(1,128)}, u32[]{:S(2)}) copy-start(s32[1,12]{1,0:T(1,128)} %param.7) | copy-start | bytes 148
  25.2 21.4 %collective-permute-start.1 = (bf16[16,1024]{1,0:T(8,128)(2,1)S(1)}, bf16[16,1024]{1,0:T(8,128)(2,1)S(1)}, u32[]{:S(2)}, u32[]{:S(2)}) collective-permute-start(bf16[16,1024]{1,0:T(8,128)(2,1)S(1)} %get-tuple-element.8), channel_id=1, source_target_pairs={{1,0},{2,1},{3,2},{4,3},{5,4},{6,5},{7,6},{8,7},{9,8},{10,9},{11,1... | collective-permute-start | bytes 98312 | tf_op jit(solution)/shard_map/ppermute | solution.py:17
  32.8 13.9 %collective-permute-start = (bf16[16,1024]{1,0:T(8,128)(2,1)S(1)}, bf16[16,1024]{1,0:T(8,128)(2,1)S(1)}, u32[]{:S(2)}, u32[]{:S(2)}) collective-permute-start(bf16[16,1024]{1,0:T(8,128)(2,1)S(1)} %get-tuple-element.7), channel_id=1, source_target_pairs={{0,1},{1,2},{2,3},{3,4},{4,5},{5,6},{6,7},{7,8},{8,9},{9,10},{10,1... | collective-permute-start | bytes 98312 | tf_op jit(solution)/shard_map/ppermute | solution.py:16
  68.6 5.3 %copy-start.1 = (bf16[64,1024]{1,0:T(8,128)(2,1)}, bf16[64,1024]{1,0:T(8,128)(2,1)S(1)}, u32[]{:S(2)}) copy-start(bf16[64,1024]{1,0:T(8,128)(2,1)S(1)} %get-tuple-element.6) | copy-start | bytes 393220
  74.0 8.2 %copy-start.2 = (bf16[64,1024]{1,0:T(8,128)(2,1)S(1)}, bf16[64,1024]{1,0:T(8,128)(2,1)}, u32[]{:S(2)}) copy-start(bf16[64,1024]{1,0:T(8,128)(2,1)} %copy-done.1) | copy-start | bytes 393220
  86.5 1.2 copy-start.19
  86.6 1.1 copy-start.18
  86.7 1.0 copy-start.17
  86.9 1.0 copy-start.16
  87.0 1.0 copy-start.15
  87.1 1.0 copy-start.14
  87.2 1.0 copy-start.13
  88.4 1.0 copy-start.11
  88.5 1.1 copy-start.9
  88.7 1.4 %copy-start.7 = (bf16[64,8,1024]{2,0,1:T(8,128)(2,1)}, bf16[64,8,1024]{2,0,1:T(8,128)(2,1)S(1)}, u32[]{:S(2)}) copy-start(bf16[64,8,1024]{2,0,1:T(8,128)(2,1)S(1)} %constant_dynamic-update-slice_fusion.24) | copy-start | bytes 3145732
  89.4 1.0 copy-start.5
  89.8 1.0 copy-start.3
  115.8 2.5 %copy-start.10 = (bf16[64,8,1024]{2,0,1:T(8,128)(2,1)S(1)}, bf16[64,8,1024]{2,0,1:T(8,128)(2,1)}, u32[]{:S(2)}) copy-start(bf16[64,8,1024]{2,0,1:T(8,128)(2,1)} %copy-done.9) | copy-start | bytes 3145732
  116.3 2.6 %copy-start.8 = (bf16[64,8,1024]{2,0,1:T(8,128)(2,1)S(1)}, bf16[64,8,1024]{2,0,1:T(8,128)(2,1)}, u32[]{:S(2)}) copy-start(bf16[64,8,1024]{2,0,1:T(8,128)(2,1)} %copy-done.7) | copy-start | bytes 3145732
  116.5 2.9 %copy-start.6 = (bf16[64,8,1024]{2,0,1:T(8,128)(2,1)S(1)}, bf16[64,8,1024]{2,0,1:T(8,128)(2,1)}, u32[]{:S(2)}) copy-start(bf16[64,8,1024]{2,0,1:T(8,128)(2,1)} %copy-done.5) | copy-start | bytes 3145732
  118.4 1.6 %copy-start.4 = (bf16[64,8,1024]{2,0,1:T(8,128)(2,1)S(1)}, bf16[64,8,1024]{2,0,1:T(8,128)(2,1)}, u32[]{:S(2)}) copy-start(bf16[64,8,1024]{2,0,1:T(8,128)(2,1)} %copy-done.3) | copy-start | bytes 3145732
Sparse Core Ops, SparseCore 0:
  74.1 39.3 all-gather.1
where the time goes:
time: 133 us; the launch traced here: 131 us
  local copies, waits for them, and re-layouts  43 us (32%)
  other arithmetic  23.2 us (17%)
  waiting for transfers between devices  22.7 us (17%)
  between operations  15.2 us (11%)
  starting transfers between devices  9.47 us (7%)
  blocking collectives  9.26 us (7%)
  matrix products  7.9 us (6%)
    all_gather x1, waiting for transfers between devices, shards(): lax.all_gather(filtered, 'chan', axis=0, tiled=True)  22.7 us
    unnamed x1, other arithmetic  21.9 us
    slice x63, local copies, waits for them, and re-layouts, correlate(): shifted.append(jnp.pad(receivers[:, lag:], ((0, 0), (0, lag))))  18.4 us
    reshape x1, local copies, waits for them, and re-layouts, fir_matrix(): return flat.reshape(length, 2 * length - 1)[:, length - 1:]  10.7 us
    squeeze x1, blocking collectives, shards(): sources = jnp.take(whole_traces, whole_index[0], axis=0)  9.26 us
    ppermute x1, starting transfers between devices, extended(): after = lax.ppermute(leading, axis, down)  7.55 us
    unnamed x111, local copies, waits for them, and re-layouts  6.9 us
    dot_general x8, matrix products, correlate(): lax.dot_general(stacked, sources, (((1,), (1,)), ((), ())), preferred_ele...  5.37 us
  transfers between devices with their start and end apart: 3, of which 1 were waited for; matrix products, arithmetic and copies ran while one was open for 12% of the time, Pallas kernels for 0%

commit v1 on v0

v1 whole, which is shorter than its diff:
```python
import functools

import jax
import jax.numpy as jnp
from jax import lax
from jax.experimental import pallas as pl
from jax.experimental.pallas import tpu as pltpu
from jax.sharding import PartitionSpec as P

LAGS = 64
MINOR = 8
SLOT = 16
LANES = 128
F32, BF16 = jnp.float32, jnp.bfloat16


def iota(shape, dim):
    return lax.broadcasted_iota(jnp.int32, shape, dim)


def dot(a, b, contract=((1,), (0,))):
    return lax.dot_general(a, b, (contract, ((), ())), preferred_element_type=F32)


def fir_block(fir_ref, line_ref):
    taps = fir_ref.shape[1]
    line_ref[...] = jnp.zeros(line_ref.shape, F32)
    line_ref[0:1, 0:taps] = fir_ref[...].astype(F32)
    wide = jnp.broadcast_to(line_ref[0:1, 0 : 2 * LANES], (2 * LANES, 2 * LANES))
    toeplitz = pltpu.roll(wide, LANES, 1, stride=1, stride_axis=0)[:, :LANES]
    flip = (iota((LANES, LANES), 0) + iota((LANES, LANES), 1) == LANES - 1).astype(F32)
    return dot(toeplitz.astype(BF16), flip.astype(BF16)).astype(BF16)


def fir(x, block, out_ref, first):
    rows, length = x.shape
    count = length // LANES
    parts = []
    for b in range(count):
        now = x[:, b * LANES : (b + 1) * LANES]
        before = x[:, (b - 1) * LANES : b * LANES] if b else jnp.zeros_like(now)
        parts.append(jnp.concatenate([before, now], axis=1))
    y = dot(jnp.concatenate(parts, axis=0), block).astype(BF16)
    for b in range(count):
        at = (count - 1 - b) * LANES
        out_ref[first : first + rows, at : at + LANES] = y[b * rows : (b + 1) * rows]


def split3(x):
    high = x.astype(BF16)
    rest = x - high.astype(F32)
    middle = rest.astype(BF16)
    low = (rest - middle.astype(F32)).astype(BF16)
    return high, middle, low


def exchange_kernel(
    sections, chans,
    index_ref, space_ref, fir_ref, raw_ref,
    gathered_ref, shifted_ref,
    line, band, halo, send, slots, halo_send, halo_recv, send_sem, recv_sem,
):
    rows, length = raw_ref.shape
    half = halo.shape[0] // 2
    sec, ch = lax.axis_index("section"), lax.axis_index("chan")
    me = sec * chans + ch
    last = sections * chans - 1
    has_prev, has_next = me > 0, me < last
    prev = jnp.maximum(me - 1, 0)
    after = jnp.minimum(me + 1, last)
    prev_id = (prev // chans, prev % chans)
    next_id = (after // chans, after % chans)

    barrier = pltpu.get_barrier_semaphore()
    for k in range(1, chans):
        pl.semaphore_signal(
            barrier, inc=1, device_id=(sec, (ch + k) % chans),
            device_id_type=pl.DeviceIdType.MESH,
        )
    cross_prev = jnp.logical_and(ch == 0, has_prev)
    cross_next = jnp.logical_and(ch == chans - 1, has_next)

    @pl.when(cross_prev)
    def _():
        pl.semaphore_signal(barrier, inc=1, device_id=prev_id, device_id_type=pl.DeviceIdType.MESH)

    @pl.when(cross_next)
    def _():
        pl.semaphore_signal(barrier, inc=1, device_id=next_id, device_id_type=pl.DeviceIdType.MESH)

    pl.semaphore_wait(
        barrier, chans - 1 + cross_prev.astype(jnp.int32) + cross_next.astype(jnp.int32)
    )

    to_next = pltpu.make_async_remote_copy(
        src_ref=raw_ref.at[rows - half : rows], dst_ref=halo.at[0:half],
        send_sem=halo_send.at[0], recv_sem=halo_recv.at[0],
        device_id=next_id, device_id_type=pl.DeviceIdType.MESH,
    )
    to_prev = pltpu.make_async_remote_copy(
        src_ref=raw_ref.at[0:half], dst_ref=halo.at[half : 2 * half],
        send_sem=halo_send.at[1], recv_sem=halo_recv.at[1],
        device_id=prev_id, device_id_type=pl.DeviceIdType.MESH,
    )

    @pl.when(has_next)
    def _():
        to_next.start()

    @pl.when(has_prev)
    def _():
        to_prev.start()

    block = fir_block(fir_ref, line)
    fir(raw_ref[...], block, band, half)

    taps = space_ref.shape[0]
    spread = rows + 2 * half
    offset = iota((rows, spread), 1) - iota((rows, spread), 0)
    mix = jnp.zeros((rows, spread), F32)
    for j in range(taps):
        mix = jnp.where(offset == j, space_ref[j], mix)
    mix = jnp.concatenate(split3(mix), axis=1)
    count = index_ref.shape[1]
    row, col = iota((SLOT, rows), 0), iota((SLOT, rows), 1)
    pick = jnp.zeros((SLOT, rows), F32)
    for i in range(count):
        chosen = jnp.logical_and(row == i, col == index_ref[0, i] - ch * rows)
        pick = jnp.where(chosen, 1.0, pick)
    source_mix = dot(pick.astype(BF16), mix).astype(BF16)

    @pl.when(has_next)
    def _():
        to_next.wait_send()

    @pl.when(has_prev)
    def _():
        to_prev.wait_send()

    @pl.when(has_prev)
    def _():
        to_next.wait_recv()

    @pl.when(jnp.logical_not(has_prev))
    def _():
        halo[0:half] = jnp.zeros((half, length), BF16)

    @pl.when(has_next)
    def _():
        to_prev.wait_recv()

    @pl.when(jnp.logical_not(has_next))
    def _():
        halo[half : 2 * half] = jnp.zeros((half, length), BF16)

    line_out = halo[...]
    count_t = length // LANES
    parts = []
    for b in range(count_t):
        now = line_out[:, b * LANES : (b + 1) * LANES]
        before = line_out[:, (b - 1) * LANES : b * LANES] if b else jnp.zeros_like(now)
        parts.append(jnp.concatenate([before, now], axis=1))
    y = dot(jnp.concatenate(parts, axis=0), block).astype(BF16)
    for b in range(count_t):
        at = (count_t - 1 - b) * LANES
        mine = y[b * 2 * half : (b + 1) * 2 * half]
        band[0:half, at : at + LANES] = mine[:half]
        band[half + rows : spread, at : at + LANES] = mine[half:]

    padded = band[...]

    def space(matrix):
        total = dot(matrix[:, 0:spread], padded)
        for i in (1, 2):
            total = total + dot(matrix[:, i * spread : (i + 1) * spread], padded)
        return total.astype(BF16)

    sources = space(source_mix)
    send[...] = sources
    copies = []
    for k in range(1, chans):
        copy = pltpu.make_async_remote_copy(
            src_ref=send, dst_ref=slots.at[ch],
            send_sem=send_sem.at[k], recv_sem=recv_sem.at[k],
            device_id=(sec, (ch + k) % chans), device_id_type=pl.DeviceIdType.MESH,
        )
        copy.start()
        copies.append(copy)
    slots[ch] = sources

    own = space(mix).astype(F32)
    keep = iota((MINOR, length), 1) >= iota((MINOR, length), 0)
    for c in range(0, rows, 2):
        pair = []
        for r in (c, c + 1):
            wide = jnp.broadcast_to(own[r : r + 1, :], (MINOR, length))
            wide = pltpu.roll(wide, 0, 1, stride=1, stride_axis=0)
            pair.append(jnp.where(keep, wide, 0.0))
        shifted_ref[c * MINOR : (c + 2) * MINOR, :] = jnp.concatenate(pair, axis=0).astype(BF16)

    for copy in copies:
        copy.wait()
    for j in range(chans):
        gathered_ref[j * SLOT : (j + 1) * SLOT, :] = slots[j]


def correlate_kernel(per, gathered_ref, shifted_ref, out_ref, weights, blocks, sems):
    slots, length = gathered_ref.shape
    rows, lags, total = out_ref.shape
    lanes = pl.cdiv(total, LANES) * LANES
    row, col = iota((lanes, slots), 0), iota((lanes, slots), 1)
    chosen = jnp.logical_and(col == row // per * SLOT + row % per, row < total)
    sources = dot(chosen.astype(F32).astype(BF16), gathered_ref[...])
    time = iota((lanes, length), 1)
    scale = 1.0 / length**0.5
    copies = []
    for k in range(lags // (2 * MINOR)):
        for h in range(2):
            shift = (2 * k + h) * MINOR
            moved = sources
            if shift:
                moved = jnp.where(time < length - shift, pltpu.roll(sources, length - shift, 1), 0.0)
            weights[k, h * lanes : (h + 1) * lanes, :] = moved.astype(BF16)
        result = dot(shifted_ref[...], weights[k], ((1,), (1,))) * scale
        low = result[:, 0:total].reshape(rows, MINOR, total)
        high = result[:, lanes : lanes + total].reshape(rows, MINOR, total)
        blocks[k] = jnp.concatenate([low, high], axis=1).astype(BF16)
        copy = pltpu.make_async_copy(
            blocks.at[k], out_ref.at[:, k * 2 * MINOR : (k + 1) * 2 * MINOR, :], sems.at[k]
        )
        copy.start()
        copies.append(copy)
    for copy in copies:
        copy.wait()


def shards(sections, chans, raw_traces, fir_taps, space_taps, source_index):
    rows, length = raw_traces.shape
    half = (space_taps.shape[0] - 1) // 2
    per = source_index.shape[1]
    total = per * chans
    lanes = -(-total // LANES) * LANES
    steps = LAGS // (2 * MINOR)
    vmem, smem = pl.BlockSpec(memory_space=pltpu.VMEM), pl.BlockSpec(memory_space=pltpu.SMEM)
    gathered, shifted = pl.pallas_call(
        functools.partial(exchange_kernel, sections, chans),
        out_shape=(
            jax.ShapeDtypeStruct((chans * SLOT, length), BF16),
            jax.ShapeDtypeStruct((rows * MINOR, length), BF16),
        ),
        in_specs=[smem, smem, vmem, vmem],
        out_specs=(vmem, vmem),
        scratch_shapes=[
            pltpu.VMEM((8, 2 * LANES), F32),
            pltpu.VMEM((rows + 2 * half, length), BF16),
            pltpu.VMEM((2 * half, length), BF16),
            pltpu.VMEM((SLOT, length), BF16),
            pltpu.VMEM((chans, SLOT, length), BF16),
            pltpu.SemaphoreType.DMA((2,)),
            pltpu.SemaphoreType.DMA((2,)),
            pltpu.SemaphoreType.DMA((chans,)),
            pltpu.SemaphoreType.DMA((chans,)),
        ],
        compiler_params=pltpu.CompilerParams(
            collective_id=0, has_side_effects=True, vmem_limit_bytes=24 * 2**20
        ),
        name="exchange",
    )(source_index, space_taps, fir_taps.reshape(1, -1), raw_traces)
    return pl.pallas_call(
        functools.partial(correlate_kernel, per),
        out_shape=jax.ShapeDtypeStruct((rows, LAGS, total), BF16),
        in_specs=[vmem, vmem],
        out_specs=pl.BlockSpec(memory_space=pl.ANY),
        scratch_shapes=[
            pltpu.VMEM((steps, 2 * lanes, length), BF16),
            pltpu.VMEM((steps, rows, 2 * MINOR, total), BF16),
            pltpu.SemaphoreType.DMA((steps,)),
        ],
        compiler_params=pltpu.CompilerParams(vmem_limit_bytes=40 * 2**20),
        name="correlate",
    )(gathered, shifted)


def solution(mesh):
    return jax.shard_map(
        functools.partial(shards, mesh.shape["section"], mesh.shape["chan"]),
        mesh=mesh,
        in_specs=(P(("section", "chan"), None), P(), P(), P("section", "chan")),
        out_specs=P(("section", "chan"), None, None),
        check_vma=False,
    )
```

time: 133 us -> 19.7 us (0.15); the launches traced: 131 us -> 19.5 us
  local copies, waits for them, and re-layouts: 43 us -> 1.59 us
  other arithmetic: 23.2 us -> 0 us
  waiting for transfers between devices: 22.7 us -> 0 us
  Pallas kernels: 0 us -> 17.9 us
  between operations: 15.2 us -> 0.02 us
  starting transfers between devices: 9.47 us -> 0 us
  blocking collectives: 9.26 us -> 0 us
  matrix products: 7.9 us -> 0 us
    all_gather x1 -> x0, waiting for transfers between devices: 22.7 us -> none  [shards(): lax.all_gather(filtered, 'chan', axis=0, tiled=True)]
    slice x67 -> x0, local copies, waits for them, and re-layouts: 22 us -> none  [the longest x63 18.4 us: correlate(): shifted.append(jnp.pad(receivers[:, lag:], ((0, 0), (0, lag))))]
    unnamed x1 -> x0, other arithmetic: 21.9 us -> none
    pallas_call x0 -> x2, Pallas kernels: none -> 17.9 us  [the longest x1 15.5 us: shards(): pl.pallas_call(functools.partial(exchange_kernel, sections, chans), out_s...]
    reshape x1 -> x0, local copies, waits for them, and re-layouts: 10.7 us -> none  [fir_matrix(): return flat.reshape(length, 2 * length - 1)[:, length - 1:]]
    ppermute x2 -> x0, starting transfers between devices: 9.47 us -> none  [the longest x1 7.55 us: extended(): after = lax.ppermute(leading, axis, down)]
    squeeze x1 -> x0, blocking collectives: 9.26 us -> none  [shards(): sources = jnp.take(whole_traces, whole_index[0], axis=0)]
    dot_general x9 -> x0, matrix products: 7.9 us -> none  [the longest x8 5.37 us: correlate(): lax.dot_general(stacked, sources, (((1,), (1,)), ((), ())), preferred_ele...]
  transfers between devices with their start and end apart: 3 -> 0, of which waited for: 1 -> 0; matrix products, arithmetic and copies ran while one was open for 12% -> 0% of each run, Pallas kernels for 0% -> 0%
where the time goes in v1:
time: 19.7 us; the launch traced here: 19.5 us
  Pallas kernels  17.9 us (91%)
  local copies, waits for them, and re-layouts  1.59 us (8%)
    pallas_call x1, Pallas kernels, shards(): pl.pallas_call(functools.partial(exchange_kernel, sections, chans), out_s...  15.5 us
    pallas_call x1, Pallas kernels, shards(): pl.pallas_call(functools.partial(correlate_kernel, per), out_shape=jax.Sh...  2.4 us
    unnamed x8, local copies, waits for them, and re-layouts  1.59 us

profile of v1, /device:TPU:1, one launch (start us, length us, event | category | flops | bytes accessed | tf_op | source)
XLA Modules:
  0.0 19.5 jit_solution(1868720824089243137)
XLA Ops:
  0.0 0.0 copy-start.1
  0.0 0.0 copy-start.2
  0.0 0.0 copy-start.3
  0.0 0.6 %copy-done.1 = s32[1,12]{1,0:T(1,128)S(1)} copy-done((s32[1,12]{1,0:T(1,128)S(1)}, s32[1,12]{1,0:T(1,128)}, u32[]{:S(2)}) %copy-start.1) | copy-done | bytes 72
  0.7 0.0 copy-done.2
  0.7 0.0 copy-done.3
  0.7 0.0 copy-start
  0.7 0.9 %copy-done = bf16[64,1024]{1,0:T(8,128)(2,1)S(1)} copy-done((bf16[64,1024]{1,0:T(8,128)(2,1)S(1)}, bf16[64,1024]{1,0:T(8,128)(2,1)}, u32[]{:S(2)}) %copy-start) | copy-done | bytes 131096
  1.6 15.5 %exchange.1 = (bf16[128,1024]{1,0:T(8,128)(2,1)S(1)}, bf16[512,1024]{1,0:T(8,128)(2,1)S(1)}) custom-call(s32[1,12]{1,0:T(1,128)S(1)} %copy-done.1, f32[33]{0:T(128)S(1)} %copy-done.2, bf16[1,64]{1,0:T(2,128)(2,1)S(1)} %bitcast.1, bf16[64,1024]{1,0:T(8,128)(2,1)S(1)} %copy-done), custom_call_target="tpu_custom_call" | custom-call | tf_op jit(solution)/shard_map/exchange/pallas_call | solution.py:245
  17.1 2.4 %correlate.1 = bf16[64,64,96]{2,1,0:T(8,128)(2,1)} custom-call(bf16[128,1024]{1,0:T(8,128)(2,1)S(1)} %get-tuple-element.7.gathered_ref, bf16[512,1024]{1,0:T(8,128)(2,1)S(1)} %get-tuple-element.8.shifted_ref), custom_call_target="tpu_custom_call" | custom-call | tf_op jit(solution)/shard_map/correlate/pallas_call | solution.py:269
Async XLA Ops:
  0.0 0.7 %copy-start.1 = (s32[1,12]{1,0:T(1,128)S(1)}, s32[1,12]{1,0:T(1,128)}, u32[]{:S(2)}) copy-start(s32[1,12]{1,0:T(1,128)} %index_ref.1) | copy-start | bytes 148
  0.0 0.7 %copy-start.2 = (f32[33]{0:T(128)S(1)}, f32[33]{0:T(128)}, u32[]{:S(2)}) copy-start(f32[33]{0:T(128)} %space_ref.1) | copy-start | bytes 400
  0.0 0.7 %copy-start.3 = (bf16[64]{0:T(256)(128)(2,1)S(1)}, bf16[64]{0:T(256)(128)(2,1)}, u32[]{:S(2)}) copy-start(bf16[64]{0:T(256)(128)(2,1)} %param.5) | copy-start | bytes 388
  0.7 0.9 %copy-start = (bf16[64,1024]{1,0:T(8,128)(2,1)S(1)}, bf16[64,1024]{1,0:T(8,128)(2,1)}, u32[]{:S(2)}) copy-start(bf16[64,1024]{1,0:T(8,128)(2,1)} %raw_ref.1) | copy-start | bytes 393220

commit v2 on v1

v2 whole, which is shorter than its diff:
```python
import functools

import jax
import jax.numpy as jnp
from jax import lax
from jax.experimental import pallas as pl
from jax.experimental.pallas import tpu as pltpu
from jax.sharding import PartitionSpec as P

LAGS = 64
MINOR = 8
SLOT = 8
LANES = 128
MESH = pl.DeviceIdType.MESH
F32, BF16 = jnp.float32, jnp.bfloat16


def iota(shape, dim):
    return lax.broadcasted_iota(jnp.int32, shape, dim)


def dot(a, b, contract=((1,), (0,))):
    return lax.dot_general(a, b, (contract, ((), ())), preferred_element_type=F32)


def fir_block(fir_ref, line_ref):
    taps = fir_ref.shape[1]
    line_ref[...] = jnp.zeros(line_ref.shape, F32)
    line_ref[0:1, 0:taps] = fir_ref[...].astype(F32)
    wide = jnp.broadcast_to(line_ref[0:1, 0 : 2 * LANES], (2 * LANES, 2 * LANES))
    toeplitz = pltpu.roll(wide, LANES, 1, stride=1, stride_axis=0)[:, :LANES]
    flip = (iota((LANES, LANES), 0) + iota((LANES, LANES), 1) == LANES - 1).astype(F32)
    return dot(toeplitz.astype(BF16), flip.astype(BF16)).astype(BF16)


def fir(x, block):
    rows, length = x.shape
    count = length // LANES
    parts = []
    for b in range(count):
        now = x[:, b * LANES : (b + 1) * LANES]
        before = x[:, (b - 1) * LANES : b * LANES] if b else jnp.zeros_like(now)
        parts.append(jnp.concatenate([before, now], axis=1))
    y = dot(jnp.concatenate(parts, axis=0), block).astype(BF16)
    return [y[b * rows : (b + 1) * rows] for b in reversed(range(count))]


def split3(x):
    high = x.astype(BF16)
    rest = x - high.astype(F32)
    middle = rest.astype(BF16)
    low = (rest - middle.astype(F32)).astype(BF16)
    return high, middle, low


def exchange_kernel(
    sections, chans,
    index_hbm, space_hbm, fir_hbm, raw_hbm,
    gathered_ref, shifted_ref,
    index_ref, space_ref, fir_ref, raw_ref, line, band, halo, own_ref,
    load_sem, halo_send, halo_recv, z_send, z_recv, x_send, x_recv,
):
    rows, length = raw_ref.shape
    half = halo.shape[0] // 2
    sec, ch = lax.axis_index("section"), lax.axis_index("chan")
    me = sec * chans + ch
    last = sections * chans - 1
    has_prev, has_next = me > 0, me < last
    prev = jnp.maximum(me - 1, 0)
    after = jnp.minimum(me + 1, last)
    prev_id = (prev // chans, prev % chans)
    next_id = (after // chans, after % chans)
    partner = ch + 1 - 2 * (ch % 2)

    barrier = pltpu.get_barrier_semaphore()
    for k in range(1, chans):
        pl.semaphore_signal(barrier, inc=1, device_id=(sec, (ch + k) % chans), device_id_type=MESH)
    cross_prev = jnp.logical_and(ch == 0, has_prev)
    cross_next = jnp.logical_and(ch == chans - 1, has_next)

    @pl.when(cross_prev)
    def _():
        pl.semaphore_signal(barrier, inc=1, device_id=prev_id, device_id_type=MESH)

    @pl.when(cross_next)
    def _():
        pl.semaphore_signal(barrier, inc=1, device_id=next_id, device_id_type=MESH)

    load_raw = pltpu.make_async_copy(raw_hbm, raw_ref, load_sem.at[0])
    load_fir = pltpu.make_async_copy(fir_hbm, fir_ref, load_sem.at[1])
    load_space = pltpu.make_async_copy(space_hbm, space_ref, load_sem.at[2])
    load_index = pltpu.make_async_copy(index_hbm, index_ref, load_sem.at[3])
    load_fir.start()
    load_raw.start()
    load_space.start()
    load_index.start()
    load_fir.wait()
    block = fir_block(fir_ref, line)

    pl.semaphore_wait(
        barrier, chans - 1 + cross_prev.astype(jnp.int32) + cross_next.astype(jnp.int32)
    )

    to_next = pltpu.make_async_remote_copy(
        src_ref=raw_hbm.at[rows - half : rows], dst_ref=halo.at[0:half],
        send_sem=halo_send.at[0], recv_sem=halo_recv.at[0],
        device_id=next_id, device_id_type=MESH,
    )
    to_prev = pltpu.make_async_remote_copy(
        src_ref=raw_hbm.at[0:half], dst_ref=halo.at[half : 2 * half],
        send_sem=halo_send.at[1], recv_sem=halo_recv.at[1],
        device_id=prev_id, device_id_type=MESH,
    )

    @pl.when(has_next)
    def _():
        to_next.start()

    @pl.when(has_prev)
    def _():
        to_prev.start()

    load_raw.wait()
    own = fir(raw_ref[...], block)
    for b, part in enumerate(own):
        band[half : half + rows, b * LANES : (b + 1) * LANES] = part

    load_space.wait()
    load_index.wait()
    taps = space_ref.shape[0]
    spread = rows + 2 * half
    offset = iota((rows, spread), 1) - iota((rows, spread), 0)
    mix = jnp.zeros((rows, spread), F32)
    for j in range(taps):
        mix = jnp.where(offset == j, space_ref[j], mix)
    mix = jnp.concatenate(split3(mix), axis=1)
    count = index_ref.shape[1]
    row, col = iota((2 * SLOT, rows), 0), iota((2 * SLOT, rows), 1)
    pick = jnp.zeros((2 * SLOT, rows), F32)
    for i in range(2 * SLOT):
        source = index_ref[0, i if i < count else i - (count - SLOT)] - ch * rows
        pick = jnp.where(jnp.logical_and(row == i, col == source), 1.0, pick)
    source_mix = dot(pick.astype(BF16), mix).astype(BF16)

    @pl.when(has_prev)
    def _():
        to_next.wait_recv()

    @pl.when(jnp.logical_not(has_prev))
    def _():
        halo[0:half] = jnp.zeros((half, length), BF16)

    @pl.when(has_next)
    def _():
        to_prev.wait_recv()

    @pl.when(jnp.logical_not(has_next))
    def _():
        halo[half : 2 * half] = jnp.zeros((half, length), BF16)

    for b, part in enumerate(fir(halo[...], block)):
        band[0:half, b * LANES : (b + 1) * LANES] = part[:half]
        band[half + rows : spread, b * LANES : (b + 1) * LANES] = part[half:]
    padded = band[...]

    def space(matrix):
        total = dot(matrix[:, 0:spread], padded)
        for i in (1, 2):
            total = total + dot(matrix[:, i * spread : (i + 1) * spread], padded)
        return total

    sources = space(source_mix)
    middle = length // 2
    tail = jnp.where(
        iota((SLOT, middle), 0) < SLOT // 2,
        sources[SLOT : 2 * SLOT, 0:middle], sources[SLOT : 2 * SLOT, middle:length],
    )
    gathered_ref[ch] = jnp.concatenate([sources[0:SLOT], tail], axis=1).astype(BF16)

    def piece(owner, target, send_sem, recv_sem):
        return pltpu.make_async_remote_copy(
            src_ref=gathered_ref.at[owner], dst_ref=gathered_ref.at[owner],
            send_sem=send_sem, recv_sem=recv_sem,
            device_id=(sec, target), device_id_type=MESH,
        )

    hops = chans // 2
    over_z = [
        piece(ch, (ch + 2 * k) % chans, z_send.at[k], z_recv.at[k]) for k in range(1, hops)
    ]
    for copy in over_z:
        copy.start()
    over_x = [piece(ch, partner, x_send.at[0], x_recv.at[0])]
    over_x[0].start()

    own_ref[...] = space(mix).astype(BF16).astype(F32)

    def shift(first, end):
        keep = iota((MINOR, length), 1) >= iota((MINOR, length), 0)
        for c in range(first, end, 2):
            pair = []
            for r in (c, c + 1):
                wide = jnp.broadcast_to(own_ref[r : r + 1, :], (MINOR, length))
                wide = pltpu.roll(wide, 0, 1, stride=1, stride_axis=0)
                pair.append(jnp.where(keep, wide, 0.0))
            joined = jnp.concatenate(pair, axis=0).astype(BF16)
            shifted_ref[c * MINOR : (c + 2) * MINOR, :] = joined

    shift(0, rows // 2)
    for k in range(1, hops):
        over_z[k - 1].wait_recv()
        owner = (ch + chans - 2 * k) % chans
        copy = piece(owner, partner, x_send.at[k], x_recv.at[k])
        copy.start()
        over_x.append(copy)
    shift(rows // 2, rows)

    @pl.when(has_next)
    def _():
        to_next.wait_send()

    @pl.when(has_prev)
    def _():
        to_prev.wait_send()

    for copy in over_z:
        copy.wait_send()
    for copy in over_x:
        copy.wait()


def correlate_kernel(per, gathered_ref, shifted_ref, out_ref, weights, blocks, sems):
    chans, _, packet = gathered_ref.shape
    length = shifted_ref.shape[1]
    middle = packet - length
    rows, lags, total = out_ref.shape
    lanes = pl.cdiv(total, LANES) * LANES
    packets = [gathered_ref[j].astype(F32) for j in range(chans)]
    packets = jnp.concatenate(packets, axis=0).astype(BF16)
    row, col = iota((lanes, chans * SLOT), 0), iota((lanes, chans * SLOT), 1)
    same = jnp.logical_and(col // SLOT == row // per, row < total)

    def choose(rank):
        chosen = jnp.logical_and(same, col % SLOT == rank)
        return chosen.astype(F32).astype(BF16)

    rank = row % per
    whole = choose(rank)
    halves = [
        choose(jnp.where(rank < SLOT, -1, rank - SLOT + h * (SLOT // 2))) for h in range(2)
    ]
    sources = jnp.concatenate(
        [
            dot(whole, packets[:, h * middle : (h + 1) * middle])
            + dot(halves[h], packets[:, length:packet])
            for h in range(2)
        ],
        axis=1,
    )
    time = iota((lanes, length), 1)
    scale = 1.0 / length**0.5
    copies = []
    for k in range(lags // (2 * MINOR)):
        for h in range(2):
            shift = (2 * k + h) * MINOR
            moved = sources
            if shift:
                moved = jnp.where(time < length - shift, pltpu.roll(sources, length - shift, 1), 0.0)
            weights[k, h * lanes : (h + 1) * lanes, :] = moved.astype(BF16)
        result = dot(shifted_ref[...], weights[k], ((1,), (1,))) * scale
        low = result[:, 0:total].reshape(rows, MINOR, total)
        high = result[:, lanes : lanes + total].reshape(rows, MINOR, total)
        blocks[k] = jnp.concatenate([low, high], axis=1).astype(BF16)
        copy = pltpu.make_async_copy(
            blocks.at[k], out_ref.at[:, k * 2 * MINOR : (k + 1) * 2 * MINOR, :], sems.at[k]
        )
        copy.start()
        copies.append(copy)
    for copy in copies:
        copy.wait()


def shards(sections, chans, raw_traces, fir_taps, space_taps, source_index):
    rows, length = raw_traces.shape
    half = (space_taps.shape[0] - 1) // 2
    per = source_index.shape[1]
    total = per * chans
    lanes = -(-total // LANES) * LANES
    steps = LAGS // (2 * MINOR)
    vmem, hbm = pl.BlockSpec(memory_space=pltpu.VMEM), pl.BlockSpec(memory_space=pltpu.HBM)
    hops = chans // 2
    gathered, shifted = pl.pallas_call(
        functools.partial(exchange_kernel, sections, chans),
        out_shape=(
            jax.ShapeDtypeStruct((chans, SLOT, length + length // 2), BF16),
            jax.ShapeDtypeStruct((rows * MINOR, length), BF16),
        ),
        in_specs=[hbm, hbm, hbm, hbm],
        out_specs=(vmem, vmem),
        scratch_shapes=[
            pltpu.SMEM(source_index.shape, jnp.int32),
            pltpu.SMEM(space_taps.shape, F32),
            pltpu.VMEM((1, fir_taps.shape[0]), BF16),
            pltpu.VMEM((rows, length), BF16),
            pltpu.VMEM((8, 2 * LANES), F32),
            pltpu.VMEM((rows + 2 * half, length), BF16),
            pltpu.VMEM((2 * half, length), BF16),
            pltpu.VMEM((rows, length), F32),
            pltpu.SemaphoreType.DMA((4,)),
            pltpu.SemaphoreType.DMA((2,)),
            pltpu.SemaphoreType.DMA((2,)),
            pltpu.SemaphoreType.DMA((hops,)),
            pltpu.SemaphoreType.DMA((hops,)),
            pltpu.SemaphoreType.DMA((hops,)),
            pltpu.SemaphoreType.DMA((hops,)),
        ],
        compiler_params=pltpu.CompilerParams(
            collective_id=0, has_side_effects=True, vmem_limit_bytes=24 * 2**20
        ),
        name="exchange",
    )(
        *(
            pltpu.with_memory_space_constraint(x, pltpu.HBM)
            for x in (source_index, space_taps, fir_taps.reshape(1, -1), raw_traces)
        )
    )
    return pl.pallas_call(
        functools.partial(correlate_kernel, per),
        out_shape=jax.ShapeDtypeStruct((rows, LAGS, total), BF16),
        in_specs=[vmem, vmem],
        out_specs=pl.BlockSpec(memory_space=pl.ANY),
        scratch_shapes=[
            pltpu.VMEM((steps, 2 * lanes, length), BF16),
            pltpu.VMEM((steps, rows, 2 * MINOR, total), BF16),
            pltpu.SemaphoreType.DMA((steps,)),
        ],
        compiler_params=pltpu.CompilerParams(vmem_limit_bytes=40 * 2**20),
        name="correlate",
    )(gathered, shifted)


def solution(mesh):
    return jax.shard_map(
        functools.partial(shards, mesh.shape["section"], mesh.shape["chan"]),
        mesh=mesh,
        in_specs=(P(("section", "chan"), None), P(), P(), P("section", "chan")),
        out_specs=P(("section", "chan"), None, None),
        check_vma=False,
    )
```

time: 19.7 us -> 20.9 us (1.061)
  the two profiles are of different devices: /device:TPU:1 before, /device:TPU:0 now
where the time goes in v2:
time: 20.9 us; the launch traced here: 20.8 us
  Pallas kernels  20.8 us (100%)
    pallas_call x1, Pallas kernels, shards(): pl.pallas_call(functools.partial(exchange_kernel, sections, chans), out_s...  18.3 us
    pallas_call x1, Pallas kernels, shards(): pl.pallas_call(functools.partial(correlate_kernel, per), out_shape=jax.Sh...  2.44 us

profile of v2, /device:TPU:0, one launch (start us, length us, event | category | flops | bytes accessed | tf_op | source)
XLA Modules:
  0.0 20.8 jit_solution(5693894682964350731)
XLA Ops:
  0.0 18.3 %exchange.1 = (bf16[8,8,1536]{2,1,0:T(8,128)(2,1)S(1)}, bf16[512,1024]{1,0:T(8,128)(2,1)S(1)}) custom-call(s32[1,12]{1,0:T(1,128)} %index_hbm.1, f32[33]{0:T(128)} %space_hbm.1, bf16[1,64]{1,0:T(2,128)(2,1)} %bitcast.1, bf16[64,1024]{1,0:T(8,128)(2,1)} %raw_hbm.1), custom_call_target="tpu_custom_call" | custom-call | tf_op jit(solution)/shard_map/exchange/pallas_call | solution.py:292
  18.3 2.4 %correlate.1 = bf16[64,64,96]{2,1,0:T(8,128)(2,1)} custom-call(bf16[8,8,1536]{2,1,0:T(8,128)(2,1)S(1)} %get-tuple-element.7.gathered_ref, bf16[512,1024]{1,0:T(8,128)(2,1)S(1)} %get-tuple-element.8.shifted_ref), custom_call_target="tpu_custom_call" | custom-call | tf_op jit(solution)/shard_map/correlate/pallas_call | solution.py:327

commit v3 on v2

--- a/solution.py
+++ b/solution.py
@@ -57,8 +57,8 @@
     sections, chans,
     index_hbm, space_hbm, fir_hbm, raw_hbm,
     gathered_ref, shifted_ref,
-    index_ref, space_ref, fir_ref, raw_ref, line, band, halo, own_ref,
-    load_sem, halo_send, halo_recv, z_send, z_recv, x_send, x_recv,
+    index_ref, space_ref, fir_ref, raw_ref, line, band, halo, own_ref, source_ref,
+    load_sem, halo_send, halo_recv, send_sem, recv_sem,
 ):
     rows, length = raw_ref.shape
     half = halo.shape[0] // 2
@@ -70,21 +70,6 @@
     after = jnp.minimum(me + 1, last)
     prev_id = (prev // chans, prev % chans)
     next_id = (after // chans, after % chans)
-    partner = ch + 1 - 2 * (ch % 2)
-
-    barrier = pltpu.get_barrier_semaphore()
-    for k in range(1, chans):
-        pl.semaphore_signal(barrier, inc=1, device_id=(sec, (ch + k) % chans), device_id_type=MESH)
-    cross_prev = jnp.logical_and(ch == 0, has_prev)
-    cross_next = jnp.logical_and(ch == chans - 1, has_next)
-
-    @pl.when(cross_prev)
-    def _():
-        pl.semaphore_signal(barrier, inc=1, device_id=prev_id, device_id_type=MESH)
-
-    @pl.when(cross_next)
-    def _():
-        pl.semaphore_signal(barrier, inc=1, device_id=next_id, device_id_type=MESH)
 
     load_raw = pltpu.make_async_copy(raw_hbm, raw_ref, load_sem.at[0])
     load_fir = pltpu.make_async_copy(fir_hbm, fir_ref, load_sem.at[1])
@@ -94,56 +79,79 @@
     load_raw.start()
     load_space.start()
     load_index.start()
-    load_fir.wait()
-    block = fir_block(fir_ref, line)
-
-    pl.semaphore_wait(
-        barrier, chans - 1 + cross_prev.astype(jnp.int32) + cross_next.astype(jnp.int32)
-    )
-
-    to_next = pltpu.make_async_remote_copy(
-        src_ref=raw_hbm.at[rows - half : rows], dst_ref=halo.at[0:half],
-        send_sem=halo_send.at[0], recv_sem=halo_recv.at[0],
-        device_id=next_id, device_id_type=MESH,
-    )
-    to_prev = pltpu.make_async_remote_copy(
-        src_ref=raw_hbm.at[0:half], dst_ref=halo.at[half : 2 * half],
-        send_sem=halo_send.at[1], recv_sem=halo_recv.at[1],
-        device_id=prev_id, device_id_type=MESH,
-    )
-
-    @pl.when(has_next)
-    def _():
-        to_next.start()
-
-    @pl.when(has_prev)
-    def _():
-        to_prev.start()
-
-    load_raw.wait()
-    own = fir(raw_ref[...], block)
-    for b, part in enumerate(own):
-        band[half : half + rows, b * LANES : (b + 1) * LANES] = part
+
+    barrier = pltpu.get_barrier_semaphore()
+    cross_prev = jnp.logical_and(ch == 0, has_prev)
+    cross_next = jnp.logical_and(ch == chans - 1, has_next)
+
+    @pl.when(cross_prev)
+    def _():
+        pl.semaphore_signal(barrier, inc=1, device_id=prev_id, device_id_type=MESH)
+
+    @pl.when(cross_next)
+    def _():
+        pl.semaphore_signal(barrier, inc=1, device_id=next_id, device_id_type=MESH)
+
+    for k in range(1, chans):
+        pl.semaphore_signal(barrier, inc=1, device_id=(sec, (ch + k) % chans), device_id_type=MESH)
 
     load_space.wait()
     load_index.wait()
     taps = space_ref.shape[0]
-    spread = rows + 2 * half
-    offset = iota((rows, spread), 1) - iota((rows, spread), 0)
-    mix = jnp.zeros((rows, spread), F32)
-    for j in range(taps):
-        mix = jnp.where(offset == j, space_ref[j], mix)
-    mix = jnp.concatenate(split3(mix), axis=1)
+
+    def mixing(width, place):
+        offset = place(iota((rows, width), 1)) - iota((rows, width), 0)
+        mix = jnp.zeros((rows, width), F32)
+        for j in range(taps):
+            mix = jnp.where(offset == j, space_ref[j], mix)
+        return jnp.concatenate(split3(mix), axis=1)
+
+    mix_own = mixing(rows, lambda col: col + half)
+    mix_halo = mixing(2 * half, lambda col: jnp.where(col < half, col, col + rows))
     count = index_ref.shape[1]
     row, col = iota((2 * SLOT, rows), 0), iota((2 * SLOT, rows), 1)
     pick = jnp.zeros((2 * SLOT, rows), F32)
     for i in range(2 * SLOT):
         source = index_ref[0, i if i < count else i - (count - SLOT)] - ch * rows
         pick = jnp.where(jnp.logical_and(row == i, col == source), 1.0, pick)
-    source_mix = dot(pick.astype(BF16), mix).astype(BF16)
+    pick = pick.astype(BF16)
+    source_own = dot(pick, mix_own).astype(BF16)
+    source_halo = dot(pick, mix_halo).astype(BF16)
+
+    load_fir.wait()
+    block = fir_block(fir_ref, line)
+    load_raw.wait()
+    for b, part in enumerate(fir(raw_ref[...], block)):
+        band[:, b * LANES : (b + 1) * LANES] = part
+    thrice = jnp.concatenate([band[...]] * 3, axis=0)
+    own_ref[...] = dot(mix_own, thrice)
+    source_ref[...] = dot(source_own, thrice)
+
+    pl.semaphore_wait(
+        barrier, chans - 1 + cross_prev.astype(jnp.int32) + cross_next.astype(jnp.int32)
+    )
+
+    to_next = pltpu.make_async_remote_copy(
+        src_ref=band.at[rows - half : rows], dst_ref=halo.at[0:half],
+        send_sem=halo_send.at[0], recv_sem=halo_recv.at[0],
+        device_id=next_id, device_id_type=MESH,
+    )
+    to_prev = pltpu.make_async_remote_copy(
+        src_ref=band.at[0:half], dst_ref=halo.at[half : 2 * half],
+        send_sem=halo_send.at[1], recv_sem=halo_recv.at[1],
+        device_id=prev_id, device_id_type=MESH,
+    )
+
+    @pl.when(has_next)
+    def _():
+        to_next.start()
 
     @pl.when(has_prev)
     def _():
+        to_prev.start()
+
+    @pl.when(has_prev)
+    def _():
         to_next.wait_recv()
 
     @pl.when(jnp.logical_not(has_prev))
@@ -158,18 +166,8 @@
     def _():
         halo[half : 2 * half] = jnp.zeros((half, length), BF16)
 
-    for b, part in enumerate(fir(halo[...], block)):
-        band[0:half, b * LANES : (b + 1) * LANES] = part[:half]
-        band[half + rows : spread, b * LANES : (b + 1) * LANES] = part[half:]
-    padded = band[...]
-
-    def space(matrix):
-        total = dot(matrix[:, 0:spread], padded)
-        for i in (1, 2):
-            total = total + dot(matrix[:, i * spread : (i + 1) * spread], padded)
-        return total
-
-    sources = space(source_mix)
+    edges = jnp.concatenate([halo[...]] * 3, axis=0)
+    sources = source_ref[...] + dot(source_halo, edges)
     middle = length // 2
     tail = jnp.where(
         iota((SLOT, middle), 0) < SLOT // 2,
@@ -177,43 +175,25 @@
     )
     gathered_ref[ch] = jnp.concatenate([sources[0:SLOT], tail], axis=1).astype(BF16)
 
-    def piece(owner, target, send_sem, recv_sem):
-        return pltpu.make_async_remote_copy(
-            src_ref=gathered_ref.at[owner], dst_ref=gathered_ref.at[owner],
-            send_sem=send_sem, recv_sem=recv_sem,
-            device_id=(sec, target), device_id_type=MESH,
+    copies = []
+    for k in sorted(range(1, chans), key=lambda k: abs(2 * k - chans)):
+        copy = pltpu.make_async_remote_copy(
+            src_ref=gathered_ref.at[ch], dst_ref=gathered_ref.at[ch],
+            send_sem=send_sem.at[k], recv_sem=recv_sem.at[k],
+            device_id=(sec, (ch + k) % chans), device_id_type=MESH,
         )
-
-    hops = chans // 2
-    over_z = [
-        piece(ch, (ch + 2 * k) % chans, z_send.at[k], z_recv.at[k]) for k in range(1, hops)
-    ]
-    for copy in over_z:
         copy.start()
-    over_x = [piece(ch, partner, x_send.at[0], x_recv.at[0])]
-    over_x[0].start()
-
-    own_ref[...] = space(mix).astype(BF16).astype(F32)
-
-    def shift(first, end):
-        keep = iota((MINOR, length), 1) >= iota((MINOR, length), 0)
-        for c in range(first, end, 2):
-            pair = []
-            for r in (c, c + 1):
-                wide = jnp.broadcast_to(own_ref[r : r + 1, :], (MINOR, length))
-                wide = pltpu.roll(wide, 0, 1, stride=1, stride_axis=0)
-                pair.append(jnp.where(keep, wide, 0.0))
-            joined = jnp.concatenate(pair, axis=0).astype(BF16)
-            shifted_ref[c * MINOR : (c + 2) * MINOR, :] = joined
-
-    shift(0, rows // 2)
-    for k in range(1, hops):
-        over_z[k - 1].wait_recv()
-        owner = (ch + chans - 2 * k) % chans
-        copy = piece(owner, partner, x_send.at[k], x_recv.at[k])
-        copy.start()
-        over_x.append(copy)
-    shift(rows // 2, rows)
+        copies.append(copy)
+
+    own_ref[...] = (own_ref[...] + dot(mix_halo, edges)).astype(BF16).astype(F32)
+    keep = iota((MINOR, length), 1) >= iota((MINOR, length), 0)
+    for c in range(0, rows, 2):
+        pair = []
+        for r in (c, c + 1):
+            wide = jnp.broadcast_to(own_ref[r : r + 1, :], (MINOR, length))
+            wide = pltpu.roll(wide, 0, 1, stride=1, stride_axis=0)
+            pair.append(jnp.where(keep, wide, 0.0))
+        shifted_ref[c * MINOR : (c + 2) * MINOR, :] = jnp.concatenate(pair, axis=0).astype(BF16)
 
     @pl.when(has_next)
     def _():
@@ -223,9 +203,7 @@
     def _():
         to_prev.wait_send()
 
-    for copy in over_z:
-        copy.wait_send()
-    for copy in over_x:
+    for copy in copies:
         copy.wait()
 
 
@@ -288,7 +266,6 @@
     lanes = -(-total // LANES) * LANES
     steps = LAGS // (2 * MINOR)
     vmem, hbm = pl.BlockSpec(memory_space=pltpu.VMEM), pl.BlockSpec(memory_space=pltpu.HBM)
-    hops = chans // 2
     gathered, shifted = pl.pallas_call(
         functools.partial(exchange_kernel, sections, chans),
         out_shape=(
@@ -303,16 +280,15 @@
             pltpu.VMEM((1, fir_taps.shape[0]), BF16),
             pltpu.VMEM((rows, length), BF16),
             pltpu.VMEM((8, 2 * LANES), F32),
-            pltpu.VMEM((rows + 2 * half, length), BF16),
+            pltpu.VMEM((rows, length), BF16),
             pltpu.VMEM((2 * half, length), BF16),
             pltpu.VMEM((rows, length), F32),
+            pltpu.VMEM((2 * SLOT, length), F32),
             pltpu.SemaphoreType.DMA((4,)),
             pltpu.SemaphoreType.DMA((2,)),
             pltpu.SemaphoreType.DMA((2,)),
-            pltpu.SemaphoreType.DMA((hops,)),
-            pltpu.SemaphoreType.DMA((hops,)),
-            pltpu.SemaphoreType.DMA((hops,)),
-            pltpu.SemaphoreType.DMA((hops,)),
+            pltpu.SemaphoreType.DMA((chans,)),
+            pltpu.SemaphoreType.DMA((chans,)),
         ],
         compiler_params=pltpu.CompilerParams(
             collective_id=0, has_side_effects=True, vmem_limit_bytes=24 * 2**20

time: 20.9 us -> 19 us (0.909)
  the two profiles are of different devices: /device:TPU:0 before, /device:TPU:1 now
where the time goes in v3:
time: 19 us; the launch traced here: 18.9 us
  Pallas kernels  18.9 us (99%)
    pallas_call x1, Pallas kernels, shards(): pl.pallas_call(functools.partial(exchange_kernel, sections, chans), out_s...  16.5 us
    pallas_call x1, Pallas kernels, shards(): pl.pallas_call(functools.partial(correlate_kernel, per), out_shape=jax.Sh...  2.44 us

profile of v3, /device:TPU:1, one launch (start us, length us, event | category | flops | bytes accessed | tf_op | source)
XLA Modules:
  0.0 18.9 jit_solution(9596134496567210605)
XLA Ops:
  0.0 16.5 %exchange.1 = (bf16[8,8,1536]{2,1,0:T(8,128)(2,1)S(1)}, bf16[512,1024]{1,0:T(8,128)(2,1)S(1)}) custom-call(s32[1,12]{1,0:T(1,128)} %index_hbm.1, f32[33]{0:T(128)} %space_hbm.1, bf16[1,64]{1,0:T(2,128)(2,1)} %bitcast.1, bf16[64,1024]{1,0:T(8,128)(2,1)} %raw_hbm.1), custom_call_target="tpu_custom_call" | custom-call | tf_op jit(solution)/shard_map/exchange/pallas_call | solution.py:269
  16.5 2.4 %correlate.1 = bf16[64,64,96]{2,1,0:T(8,128)(2,1)} custom-call(bf16[8,8,1536]{2,1,0:T(8,128)(2,1)S(1)} %get-tuple-element.7.gathered_ref, bf16[512,1024]{1,0:T(8,128)(2,1)S(1)} %get-tuple-element.8.shifted_ref), custom_call_target="tpu_custom_call" | custom-call | tf_op jit(solution)/shard_map/correlate/pallas_call | solution.py:303

commit v4 on v3

--- a/solution.py
+++ b/solution.py
@@ -176,7 +176,7 @@
     gathered_ref[ch] = jnp.concatenate([sources[0:SLOT], tail], axis=1).astype(BF16)
 
     copies = []
-    for k in sorted(range(1, chans), key=lambda k: abs(2 * k - chans)):
+    for k in range(1, chans):
         copy = pltpu.make_async_remote_copy(
             src_ref=gathered_ref.at[ch], dst_ref=gathered_ref.at[ch],
             send_sem=send_sem.at[k], recv_sem=recv_sem.at[k],

time: 19 us -> 17.1 us (0.900)
  Pallas kernels: 18.9 us -> 16.9 us
    pallas_call x1, Pallas kernels: 16.5 us -> 14.5 us  [shards(): pl.pallas_call(functools.partial(exchange_kernel, sections, chans), out_s...]
where the time goes in v4:
time: 17.1 us; the launch traced here: 16.9 us
  Pallas kernels  16.9 us (99%)
    pallas_call x1, Pallas kernels, shards(): pl.pallas_call(functools.partial(exchange_kernel, sections, chans), out_s...  14.5 us
    pallas_call x1, Pallas kernels, shards(): pl.pallas_call(functools.partial(correlate_kernel, per), out_shape=jax.Sh...  2.45 us

profile of v4, /device:TPU:1, one launch (start us, length us, event | category | flops | bytes accessed | tf_op | source)
XLA Modules:
  0.0 16.9 jit_solution(11233911851067956086)
XLA Ops:
  0.0 14.5 %exchange.1 = (bf16[8,8,1536]{2,1,0:T(8,128)(2,1)S(1)}, bf16[512,1024]{1,0:T(8,128)(2,1)S(1)}) custom-call(s32[1,12]{1,0:T(1,128)} %index_hbm.1, f32[33]{0:T(128)} %space_hbm.1, bf16[1,64]{1,0:T(2,128)(2,1)} %bitcast.1, bf16[64,1024]{1,0:T(8,128)(2,1)} %raw_hbm.1), custom_call_target="tpu_custom_call" | custom-call | tf_op jit(solution)/shard_map/exchange/pallas_call | solution.py:269
  14.5 2.4 %correlate.1 = bf16[64,64,96]{2,1,0:T(8,128)(2,1)} custom-call(bf16[8,8,1536]{2,1,0:T(8,128)(2,1)S(1)} %get-tuple-element.7.gathered_ref, bf16[512,1024]{1,0:T(8,128)(2,1)S(1)} %get-tuple-element.8.shifted_ref), custom_call_target="tpu_custom_call" | custom-call | tf_op jit(solution)/shard_map/correlate/pallas_call | solution.py:303

commit v5 on v4

--- a/solution.py
+++ b/solution.py
@@ -215,17 +215,18 @@
     lanes = pl.cdiv(total, LANES) * LANES
     packets = [gathered_ref[j].astype(F32) for j in range(chans)]
     packets = jnp.concatenate(packets, axis=0).astype(BF16)
-    row, col = iota((lanes, chans * SLOT), 0), iota((lanes, chans * SLOT), 1)
-    same = jnp.logical_and(col // SLOT == row // per, row < total)
-
-    def choose(rank):
-        chosen = jnp.logical_and(same, col % SLOT == rank)
-        return chosen.astype(F32).astype(BF16)
-
-    rank = row % per
-    whole = choose(rank)
+    row, col = iota((total, chans * SLOT), 0), iota((total, chans * SLOT), 1)
+    inside = jnp.bitwise_and(col, SLOT - 1)
+    rank = row - (lax.shift_right_logical(col, SLOT.bit_length() - 1)) * per - inside
+    early = inside < SLOT // 2
+
+    def choose(chosen):
+        return jnp.where(chosen, 1.0, 0.0).astype(BF16)
+
+    whole = choose(rank == 0)
     halves = [
-        choose(jnp.where(rank < SLOT, -1, rank - SLOT + h * (SLOT // 2))) for h in range(2)
+        choose(jnp.logical_and(rank == SLOT, early)),
+        choose(jnp.logical_and(rank == SLOT // 2, jnp.logical_not(early))),
     ]
     sources = jnp.concatenate(
         [
@@ -235,16 +236,22 @@
         ],
         axis=1,
     )
-    time = iota((lanes, length), 1)
+    edge = iota((total, LANES), 1)
     scale = 1.0 / length**0.5
+    if lanes > total:
+        for h in range(2):
+            fill = jnp.zeros((weights.shape[0], lanes - total, length), BF16)
+            weights[:, h * lanes + total : (h + 1) * lanes, :] = fill
     copies = []
     for k in range(lags // (2 * MINOR)):
         for h in range(2):
             shift = (2 * k + h) * MINOR
             moved = sources
             if shift:
-                moved = jnp.where(time < length - shift, pltpu.roll(sources, length - shift, 1), 0.0)
-            weights[k, h * lanes : (h + 1) * lanes, :] = moved.astype(BF16)
+                moved = pltpu.roll(sources, length - shift, 1)
+                tail = jnp.where(edge < LANES - shift, moved[:, length - LANES :], 0.0)
+                moved = jnp.concatenate([moved[:, : length - LANES], tail], axis=1)
+            weights[k, h * lanes : h * lanes + total, :] = moved.astype(BF16)
         result = dot(shifted_ref[...], weights[k], ((1,), (1,))) * scale
         low = result[:, 0:total].reshape(rows, MINOR, total)
         high = result[:, lanes : lanes + total].reshape(rows, MINOR, total)

time: 17.1 us -> 17 us (level)
  no operation moved by 1% of the time
where the time goes in v5:
time: 17 us; the launch traced here: 16.9 us
  Pallas kernels  16.9 us (99%)
    pallas_call x1, Pallas kernels, shards(): pl.pallas_call(functools.partial(exchange_kernel, sections, chans), out_s...  14.5 us
    pallas_call x1, Pallas kernels, shards(): pl.pallas_call(functools.partial(correlate_kernel, per), out_shape=jax.Sh...  2.4 us

profile of v5, /device:TPU:1, one launch (start us, length us, event | category | flops | bytes accessed | tf_op | source)
XLA Modules:
  0.0 16.9 jit_solution(12754241007279090776)
XLA Ops:
  0.0 14.5 %exchange.1 = (bf16[8,8,1536]{2,1,0:T(8,128)(2,1)S(1)}, bf16[512,1024]{1,0:T(8,128)(2,1)S(1)}) custom-call(s32[1,12]{1,0:T(1,128)} %index_hbm.1, f32[33]{0:T(128)} %space_hbm.1, bf16[1,64]{1,0:T(2,128)(2,1)} %bitcast.1, bf16[64,1024]{1,0:T(8,128)(2,1)} %raw_hbm.1), custom_call_target="tpu_custom_call" | custom-call | tf_op jit(solution)/shard_map/exchange/pallas_call | solution.py:276
  14.5 2.4 %correlate.1 = bf16[64,64,96]{2,1,0:T(8,128)(2,1)} custom-call(bf16[8,8,1536]{2,1,0:T(8,128)(2,1)S(1)} %get-tuple-element.7.gathered_ref, bf16[512,1024]{1,0:T(8,128)(2,1)S(1)} %get-tuple-element.8.shifted_ref), custom_call_target="tpu_custom_call" | custom-call | tf_op jit(solution)/shard_map/correlate/pallas_call | solution.py:310
